TPU v7x, 512 devices: a whole 4x4x16 slice. The times are simulated.
512 devices in a mesh: space: 64 (over x, z), node: 4 (over y_hi, core), tm: 2 (over y_lo).
Axes of the slice: x: 4, y: 4 (y_hi: 2, y_lo: 2; y = y_hi * 2 + y_lo), z: 16, core: 2. Of those that a mesh axis runs over, the one named last changes fastest.
Arguments:
- start_old: float32 [2, 512, 128, 256], P('tm', 'space'), may hold values from -4 to 4
- nodes_old: float32 [2, 4, 512, 128, 256], P('tm', 'node', 'space'), may hold values from -4 to 4
Outputs:
- nodes_new: float32 [2, 4, 512, 128, 256], P('tm', 'node', 'space')
- end_new: float32 [2, 512, 128, 256], P('tm', 'space')
All inputs are finite; a program needn't handle non-finite values.
Results may differ from a plain program's by a relative error of at most 0.00002.
Values sent between devices are 32-bit elements; how exact they have to be, the bound alone decides.
A program may use at most 64 MiB of HBM per device.

v0:
```python
import jax
import jax.numpy as jnp
from jax import lax
from jax.sharding import PartitionSpec as P

NODES = 4
PASSES = 4


time_step = 0.25
diffusion = 4.0
reaction = 1.0


def padded_2(block, sides, width):
    for axis, dim in sides:
        count = lax.axis_size(axis)
        forward = [(i, i + 1) for i in range(count - 1)]
        forward.append((count - 1, 0))
        backward = [(target, source) for source, target in forward]
        low = lax.ppermute(
            lax.slice_in_dim(block, block.shape[dim] - width, None, axis=dim), axis, forward
        )
        high = lax.ppermute(lax.slice_in_dim(block, 0, width, axis=dim), axis, backward)
        block = jnp.concatenate([low, block, high], axis=dim)
    return block


def shifted_2(array, axis, by):
    size = lax.axis_size(axis)
    pairs = [(i, i + by) for i in range(size) if 0 <= i + by < size]
    return lax.ppermute(array, axis, pairs)


def collocation(count):
    points = [-0.8611363115940526, -0.3399810435848563, 0.3399810435848563, 0.8611363115940526]
    raw_weights = [0.3478548451374538, 0.6521451548625461, 0.6521451548625461, 0.3478548451374538]
    node_times = [(point + 1.0) / 2.0 for point in points]
    quadrature = [[0.0 for column in range(count)] for target in range(count)]
    for source in range(count):
        coeffs = [1.0]
        scaling = 1.0
        for other in range(count):
            if other != source:
                other_time = node_times[other]
                shifted = [0.0] + coeffs
                for power in range(len(coeffs)):
                    shifted[power] = shifted[power] - other_time * coeffs[power]
                coeffs = shifted
                scaling = scaling * (node_times[source] - other_time)
        for target in range(count):
            target_time = node_times[target]
            integral = 0.0
            for power in range(len(coeffs)):
                integral = integral + coeffs[power] * target_time ** (power + 1) / (power + 1)
            quadrature[target][source] = integral / scaling
    return (node_times, quadrature, [weight / 2.0 for weight in raw_weights])


def neighbour_sum(padded):
    inner = padded[1:-1]
    total = padded[2:] + padded[:-2]
    total = total + jnp.roll(inner, -1, 1) + jnp.roll(inner, 1, 1)
    total = total + jnp.roll(inner, -1, 2) + jnp.roll(inner, 1, 2)
    return total


def forcing(values, padded):
    laplace = neighbour_sum(padded) - 6.0 * values
    return (laplace, diffusion * laplace + reaction * (values - values * values * values))


def on_device(start_old, nodes_old):
    node_times, quadrature, weights = collocation(NODES)
    node_index = lax.axis_index("node")
    node_time = jnp.asarray(node_times, jnp.float32)[node_index]
    weight_table = jnp.asarray(weights, jnp.float32)
    node_weight = weight_table[node_index]
    quad_table = jnp.asarray(quadrature, jnp.float32)
    state_old = nodes_old[0, 0]
    start_state = start_old[0]
    padded = padded_2(state_old, (("space", 0),), 1)
    laplace_old, force_old = forcing(state_old, padded)
    quad_row = quad_table[node_index]
    shard_piece = lax.all_gather(force_old[None], "node", axis=0, tiled=True)
    quad_part = jnp.sum(quad_row[:, None, None, None] * shard_piece, axis=0)
    weight_part = jnp.sum(weight_table[:, None, None, None] * shard_piece, axis=0)
    end_old = start_state + time_step * weight_part
    received = shifted_2(end_old, "tm", 1)
    begin_state = jnp.where(lax.axis_index("tm") == 0, start_state, received)
    implicit = time_step * diffusion * node_time
    right_side = begin_state + time_step * quad_part - implicit * laplace_old
    divisor = 1.0 + 6.0 * implicit
    iterate = state_old
    for step_index in range(PASSES):
        widened = padded_2(iterate, (("space", 0),), 1)
        iterate = (right_side + implicit * neighbour_sum(widened)) / divisor
    padded_new = padded_2(iterate, (("space", 0),), 1)
    laplace_new, force_new = forcing(iterate, padded_new)
    weighted_new = lax.psum(node_weight * force_new, "node")
    end_new = begin_state + time_step * weighted_new
    return (iterate[None, None], end_new[None])


def solution(mesh):
    return jax.shard_map(
        on_device,
        mesh=mesh,
        in_specs=(P("tm", "space", None, None), P("tm", "node", "space", None, None)),
        out_specs=(P("tm", "node", "space", None, None), P("tm", "space", None, None)),
        check_vma=False,
    )
```

profile of v0, /device:TPU:1, one launch (start us, length us, event | category | flops | bytes accessed | tf_op | source)
XLA Modules:
  0.0 228.6 jit_solution(15902153033855880192)
XLA Ops:
  7.2 1.1 slice_bitcast_fusion.1
  8.3 14.1 %collective-permute-start = (f32[1,128,256]{2,1,0:T(8,128)S(1)}, f32[1,128,256]{2,1,0:T(8,128)S(1)}, u32[]{:S(2)}, u32[]{:S(2)}) collective-permute-start(f32[1,128,256]{2,1,0:T(8,128)S(1)} %get-tuple-element.48), channel_id=1, source_target_pairs={{8,0},{16,8},{24,16},{32,24},{40,32},{48,40},{56,48},{64,56},{72,6... | collective-permute-start | bytes 393224 | tf_op jit(solution)/shard_map/ppermute | solution.py:24
  22.4 1.9 collective-permute-start.1
  24.4 1.4 fusion.63
  25.8 1.9 fusion.62
  27.7 0.2 fusion.60
  27.9 3.5 %collective-permute-done.1 = f32[1,128,256]{2,1,0:T(8,128)S(1)} collective-permute-done((f32[1,128,256]{2,1,0:T(8,128)S(1)}, f32[1,128,256]{2,1,0:T(8,128)S(1)}, u32[]{:S(2)}, u32[]{:S(2)}) %collective-permute-start.1) | collective-permute-done | bytes 131104 | tf_op jit(solution)/shard_map/ppermute | solution.py:21
  31.5 2.2 fusion
  33.8 0.8 dynamic-slice_bitcast_fusion
  34.5 38.3 %all-gather.3.cloned.1.call-done = f32[32,128,256]{2,1,0:T(8,128)} async-done(((f32[8,128,256]{2,1,0:T(8,128)}), f32[32,128,256]{2,1,0:T(8,128)}) %all-gather.3.cloned.1.call-update) | async-done | bytes 4194320 | tf_op jit(solution)/shard_map/all_gather | solution.py:85
  72.8 4.1 %multiply_reduce_fusion.1 = (f32[8,128,256]{2,1,0:T(8,128)S(1)}, f32[8,128,256]{2,1,0:T(8,128)}) fusion(f32[4,8,128,256]{3,2,1,0:T(8,128)} %bitcast.30, f32[4]{0:T(128)S(1)} %copy-done.3, f32[4]{0:T(128)S(1)} %dynamic-slice_bitcast_fusion), kind=kLoop, calls=%fused_computation.1 | loop fusion | flops 3670016 | bytes 6291488 | tf_op jit(solution)/shard_map/reduce_sum | solution.py:87
  76.9 1.1 bitcast_add_fusion
  78.0 2.3 collective-permute-start.2
  80.3 0.7 dynamic_slice.11
  81.0 0.6 dynamic_slice.10
  82.1 20.7 %collective-permute-done.2 = f32[8,128,256]{2,1,0:T(8,128)S(1)} collective-permute-done((f32[8,128,256]{2,1,0:T(8,128)}, f32[8,128,256]{2,1,0:T(8,128)S(1)}, u32[]{:S(2)}, u32[]{:S(2)}) %collective-permute-start.2) | collective-permute-done | bytes 1048608 | tf_op jit(solution)/shard_map/ppermute | solution.py:32
  102.8 2.5 %add_divide_fusion = (f32[8,128,256]{2,1,0:T(8,128)S(1)}, f32[8,128,256]{2,1,0:T(8,128)S(1)}) fusion(f32[8,128,256]{2,1,0:T(8,128)} %get-tuple-element.7, f32[]{:T(128)S(6)} %add.127, f32[]{:T(128)} %bitcast.6, f32[1,1,8,128,256]{4,3,2,1,0:T(8,128)S(1)} %copy-done, f32[8,128,256]{2,1,0:T(8,128)} %get-tuple-element.3, ...), kind=kLoop, calls=%fused_computation.56 | loop fusion | flops 2621440 | bytes 7340041 | tf_op jit(solution)/shard_map/div | solution.py:97
  105.3 0.2 fusion.55
  105.5 0.2 fusion.58
  105.7 0.4 fusion.56
  106.0 7.8 %collective-permute-start.3 = (f32[1,128,256]{2,1,0:T(8,128)S(1)}, f32[1,128,256]{2,1,0:T(8,128)S(1)}, u32[]{:S(2)}, u32[]{:S(2)}) collective-permute-start(f32[1,128,256]{2,1,0:T(8,128)S(1)} %get-tuple-element.46), channel_id=1, source_target_pairs={{8,0},{16,8},{24,16},{32,24},{40,32},{48,40},{56,48},{64,56},{72,6... | collective-permute-start | bytes 393224 | tf_op jit(solution)/shard_map/ppermute | solution.py:24
  113.9 1.9 collective-permute-start.4
  115.8 7.1 %collective-permute-done.4 = f32[1,128,256]{2,1,0:T(8,128)S(1)} collective-permute-done((f32[1,128,256]{2,1,0:T(8,128)S(1)}, f32[1,128,256]{2,1,0:T(8,128)S(1)}, u32[]{:S(2)}, u32[]{:S(2)}) %collective-permute-start.4) | collective-permute-done | bytes 131104 | tf_op jit(solution)/shard_map/ppermute | solution.py:21
  122.9 1.2 fusion.33
  124.1 0.2 fusion.50
  124.3 0.2 fusion.53
  124.5 0.4 fusion.51
  124.9 1.9 collective-permute-start.5
  126.8 3.4 %collective-permute-start.6 = (f32[1,128,256]{2,1,0:T(8,128)S(1)}, f32[1,128,256]{2,1,0:T(8,128)S(1)}, u32[]{:S(2)}, u32[]{:S(2)}) collective-permute-start(f32[1,128,256]{2,1,0:T(8,128)S(1)} %get-tuple-element.37), channel_id=1, source_target_pairs={{0,8},{8,16},{16,24},{24,32},{32,40},{40,48},{48,56},{56,64},{64,7... | collective-permute-start | bytes 393224 | tf_op jit(solution)/shard_map/ppermute | solution.py:21
  130.2 0.4 collective-permute-done.5
  130.6 5.2 %collective-permute-done.6 = f32[1,128,256]{2,1,0:T(8,128)S(1)} collective-permute-done((f32[1,128,256]{2,1,0:T(8,128)S(1)}, f32[1,128,256]{2,1,0:T(8,128)S(1)}, u32[]{:S(2)}, u32[]{:S(2)}) %collective-permute-start.6) | collective-permute-done | bytes 131104 | tf_op jit(solution)/shard_map/ppermute | solution.py:21
  135.9 1.2 fusion.25
  137.1 0.2 fusion.45
  137.5 0.4 fusion.46
  137.9 1.9 collective-permute-start.7
  139.8 3.4 %collective-permute-start.8 = (f32[1,128,256]{2,1,0:T(8,128)S(1)}, f32[1,128,256]{2,1,0:T(8,128)S(1)}, u32[]{:S(2)}, u32[]{:S(2)}) collective-permute-start(f32[1,128,256]{2,1,0:T(8,128)S(1)} %get-tuple-element.27), channel_id=1, source_target_pairs={{0,8},{8,16},{16,24},{24,32},{32,40},{40,48},{48,56},{56,64},{64,7... | collective-permute-start | bytes 393224 | tf_op jit(solution)/shard_map/ppermute | solution.py:21
  143.2 0.4 collective-permute-done.7
  143.6 5.2 %collective-permute-done.8 = f32[1,128,256]{2,1,0:T(8,128)S(1)} collective-permute-done((f32[1,128,256]{2,1,0:T(8,128)S(1)}, f32[1,128,256]{2,1,0:T(8,128)S(1)}, u32[]{:S(2)}, u32[]{:S(2)}) %collective-permute-start.8) | collective-permute-done | bytes 131104 | tf_op jit(solution)/shard_map/ppermute | solution.py:21
  148.8 1.2 fusion.17
  150.1 0.2 fusion.40
  150.5 0.4 fusion.41
  150.9 1.9 collective-permute-start.9
  152.8 3.4 %collective-permute-start.10 = (f32[1,128,256]{2,1,0:T(8,128)S(1)}, f32[1,128,256]{2,1,0:T(8,128)S(1)}, u32[]{:S(2)}, u32[]{:S(2)}) collective-permute-start(f32[1,128,256]{2,1,0:T(8,128)S(1)} %get-tuple-element.17), channel_id=1, source_target_pairs={{0,8},{8,16},{16,24},{24,32},{32,40},{40,48},{48,56},{56,64},{64,7... | collective-permute-start | bytes 393224 | tf_op jit(solution)/shard_map/ppermute | solution.py:21
  156.2 0.4 collective-permute-done.9
  156.6 5.2 %collective-permute-done.10 = f32[1,128,256]{2,1,0:T(8,128)S(1)} collective-permute-done((f32[1,128,256]{2,1,0:T(8,128)S(1)}, f32[1,128,256]{2,1,0:T(8,128)S(1)}, u32[]{:S(2)}, u32[]{:S(2)}) %collective-permute-start.10) | collective-permute-done | bytes 131104 | tf_op jit(solution)/shard_map/ppermute | solution.py:21
  161.8 2.4 %fusion.2 = f32[8,128,256]{2,1,0:T(8,128)} fusion(f32[8,128,256]{2,1,0:T(8,128)S(1)} %fusion.17, f32[1,128,256]{2,1,0:T(8,128)S(1)} %collective-permute-done.10, f32[1,128,256]{2,1,0:T(8,128)S(1)} %collective-permute-done.9, f32[8,1,256]{2,1,0:T(1,128)S(1)} %get-tuple-element.13, f32[8,127,256]{2,1,0:T(8,128)S(1)} %get-tuple-element.15, ...), kind=kLoop, calls=%fused_computation.6 | loop fusion | flops 4980736 | bytes 6553604 | tf_op jit(solution)/shard_map/mul | solution.py:100
  164.3 55.1 %all-reduce.2.cloned.1.call-done = f32[8,128,256]{2,1,0:T(8,128)} async-done(((f32[8,128,256]{2,1,0:T(8,128)}), f32[8,128,256]{2,1,0:T(8,128)}) %all-reduce.2.cloned.1.call-update) | async-done | bytes 1048592 | tf_op jit(solution)/shard_map/psum | solution.py:100
  219.4 2.4 %add_bitcast_fusion = f32[1,8,128,256]{3,2,1,0:T(8,128)} fusion(f32[8,128,256]{2,1,0:T(8,128)} %all-reduce.2.cloned.1.call-done, f32[8,128,256]{2,1,0:T(8,128)S(1)} %collective-permute-done.2, f32[1,8,128,256]{3,2,1,0:T(8,128)S(1)} %copy-done.2, pred[]{:T(512)S(6)} %eq.3), kind=kLoop, calls=%fused_computation.55 | loop fusion | flops 786432 | bytes 4194305 | tf_op jit(solution)/shard_map/broadcast_in_dim | solution.py:102
  (27 shorter events, 0.7 us)
Async XLA Ops:
  7.2 20.5 %copy-start = (f32[1,1,8,128,256]{4,3,2,1,0:T(8,128)S(1)}, f32[1,1,8,128,256]{4,3,2,1,0:T(8,128)}, u32[]{:S(2)}) copy-start(f32[1,1,8,128,256]{4,3,2,1,0:T(8,128)} %param.6) | copy-start | bytes 3145732
  7.2 65.7 %all-gather.3.cloned.1.call-start = ((), (), s32[]{:S(2)}) async-start(), calls=%async_computation.1 | async-start | bytes 5242880 | tf_op jit(solution)/shard_map/all_gather | solution.py:85
  8.3 19.6 %collective-permute-start = (f32[1,128,256]{2,1,0:T(8,128)S(1)}, f32[1,128,256]{2,1,0:T(8,128)S(1)}, u32[]{:S(2)}, u32[]{:S(2)}) collective-permute-start(f32[1,128,256]{2,1,0:T(8,128)S(1)} %get-tuple-element.48), channel_id=1, source_target_pairs={{8,0},{16,8},{24,16},{32,24},{40,32},{48,40},{56,48},{64,56},{72,6... | collective-permute-start | bytes 393224 | tf_op jit(solution)/shard_map/ppermute | solution.py:24
  22.4 9.0 %collective-permute-start.1 = (f32[1,128,256]{2,1,0:T(8,128)S(1)}, f32[1,128,256]{2,1,0:T(8,128)S(1)}, u32[]{:S(2)}, u32[]{:S(2)}) collective-permute-start(f32[1,128,256]{2,1,0:T(8,128)S(1)} %get-tuple-element.49), channel_id=1, source_target_pairs={{0,8},{8,16},{16,24},{24,32},{32,40},{40,48},{48,56},{56,64},{64,7... | collective-permute-start | bytes 393224 | tf_op jit(solution)/shard_map/ppermute | solution.py:21
  31.5 41.4 %copy-start.3 = (f32[4]{0:T(128)S(1)}, f32[4]{0:T(128)}, u32[]{:S(2)}) copy-start(f32[4]{0:T(128)} %constant.30.clone) | copy-start | bytes 52
  33.7 43.2 %copy-start.2 = (f32[1,8,128,256]{3,2,1,0:T(8,128)S(1)}, f32[1,8,128,256]{3,2,1,0:T(8,128)}, u32[]{:S(2)}) copy-start(f32[1,8,128,256]{3,2,1,0:T(8,128)} %param.5) | copy-start | bytes 3145732
  33.7 185.7 %all-reduce.2.cloned.1.call-start = ((), (), s32[]{:S(2)}) async-start(), calls=%async_computation | async-start | bytes 2097152 | tf_op jit(solution)/shard_map/psum | solution.py:100
  72.8 8.1 %copy-start.4 = (f32[4]{0:T(128)S(1)}, f32[4]{0:T(128)}, u32[]{:S(2)}) copy-start(f32[4]{0:T(128)} %constant.29.clone) | copy-start | bytes 52
  78.0 24.7 %collective-permute-start.2 = (f32[8,128,256]{2,1,0:T(8,128)}, f32[8,128,256]{2,1,0:T(8,128)S(1)}, u32[]{:S(2)}, u32[]{:S(2)}) collective-permute-start(f32[8,128,256]{2,1,0:T(8,128)} %bitcast_add_fusion), channel_id=1, source_target_pairs={{0,1},{2,3},{4,5},{6,7},{8,9},{10,11},{12,13},{14,15},{16,17},{18,... | collective-permute-start | bytes 3145736 | tf_op jit(solution)/shard_map/ppermute | solution.py:32
  106.0 9.8 %collective-permute-start.3 = (f32[1,128,256]{2,1,0:T(8,128)S(1)}, f32[1,128,256]{2,1,0:T(8,128)S(1)}, u32[]{:S(2)}, u32[]{:S(2)}) collective-permute-start(f32[1,128,256]{2,1,0:T(8,128)S(1)} %get-tuple-element.46), channel_id=1, source_target_pairs={{8,0},{16,8},{24,16},{32,24},{40,32},{48,40},{56,48},{64,56},{72,6... | collective-permute-start | bytes 393224 | tf_op jit(solution)/shard_map/ppermute | solution.py:24
  113.9 9.0 %collective-permute-start.4 = (f32[1,128,256]{2,1,0:T(8,128)S(1)}, f32[1,128,256]{2,1,0:T(8,128)S(1)}, u32[]{:S(2)}, u32[]{:S(2)}) collective-permute-start(f32[1,128,256]{2,1,0:T(8,128)S(1)} %get-tuple-element.47), channel_id=1, source_target_pairs={{0,8},{8,16},{16,24},{24,32},{32,40},{40,48},{48,56},{56,64},{64,7... | collective-permute-start | bytes 393224 | tf_op jit(solution)/shard_map/ppermute | solution.py:21
  124.9 5.7 %collective-permute-start.5 = (f32[1,128,256]{2,1,0:T(8,128)S(1)}, f32[1,128,256]{2,1,0:T(8,128)S(1)}, u32[]{:S(2)}, u32[]{:S(2)}) collective-permute-start(f32[1,128,256]{2,1,0:T(8,128)S(1)} %get-tuple-element.36), channel_id=1, source_target_pairs={{8,0},{16,8},{24,16},{32,24},{40,32},{48,40},{56,48},{64,56},{72,6... | collective-permute-start | bytes 393224 | tf_op jit(solution)/shard_map/ppermute | solution.py:24
  126.8 9.0 %collective-permute-start.6 = (f32[1,128,256]{2,1,0:T(8,128)S(1)}, f32[1,128,256]{2,1,0:T(8,128)S(1)}, u32[]{:S(2)}, u32[]{:S(2)}) collective-permute-start(f32[1,128,256]{2,1,0:T(8,128)S(1)} %get-tuple-element.37), channel_id=1, source_target_pairs={{0,8},{8,16},{16,24},{24,32},{32,40},{40,48},{48,56},{56,64},{64,7... | collective-permute-start | bytes 393224 | tf_op jit(solution)/shard_map/ppermute | solution.py:21
  137.9 5.7 %collective-permute-start.7 = (f32[1,128,256]{2,1,0:T(8,128)S(1)}, f32[1,128,256]{2,1,0:T(8,128)S(1)}, u32[]{:S(2)}, u32[]{:S(2)}) collective-permute-start(f32[1,128,256]{2,1,0:T(8,128)S(1)} %get-tuple-element.26), channel_id=1, source_target_pairs={{8,0},{16,8},{24,16},{32,24},{40,32},{48,40},{56,48},{64,56},{72,6... | collective-permute-start | bytes 393224 | tf_op jit(solution)/shard_map/ppermute | solution.py:24
  139.8 9.0 %collective-permute-start.8 = (f32[1,128,256]{2,1,0:T(8,128)S(1)}, f32[1,128,256]{2,1,0:T(8,128)S(1)}, u32[]{:S(2)}, u32[]{:S(2)}) collective-permute-start(f32[1,128,256]{2,1,0:T(8,128)S(1)} %get-tuple-element.27), channel_id=1, source_target_pairs={{0,8},{8,16},{16,24},{24,32},{32,40},{40,48},{48,56},{56,64},{64,7... | collective-permute-start | bytes 393224 | tf_op jit(solution)/shard_map/ppermute | solution.py:21
  150.1 11.8 %copy-start.1 = (f32[8,128,256]{2,1,0:T(8,128)}, f32[8,128,256]{2,1,0:T(8,128)S(1)}, u32[]{:S(2)}) copy-start(f32[8,128,256]{2,1,0:T(8,128)S(1)} %fusion.17) | copy-start | bytes 3145732
  150.9 5.7 %collective-permute-start.9 = (f32[1,128,256]{2,1,0:T(8,128)S(1)}, f32[1,128,256]{2,1,0:T(8,128)S(1)}, u32[]{:S(2)}, u32[]{:S(2)}) collective-permute-start(f32[1,128,256]{2,1,0:T(8,128)S(1)} %get-tuple-element.16), channel_id=1, source_target_pairs={{8,0},{16,8},{24,16},{32,24},{40,32},{48,40},{56,48},{64,56},{72,6... | collective-permute-start | bytes 393224 | tf_op jit(solution)/shard_map/ppermute | solution.py:24
  152.8 9.0 %collective-permute-start.10 = (f32[1,128,256]{2,1,0:T(8,128)S(1)}, f32[1,128,256]{2,1,0:T(8,128)S(1)}, u32[]{:S(2)}, u32[]{:S(2)}) collective-permute-start(f32[1,128,256]{2,1,0:T(8,128)S(1)} %get-tuple-element.17), channel_id=1, source_target_pairs={{0,8},{8,16},{16,24},{24,32},{32,40},{40,48},{48,56},{56,64},{64,7... | collective-permute-start | bytes 393224 | tf_op jit(solution)/shard_map/ppermute | solution.py:21
Sparse Core Ops, SparseCore 0:
  33.8 38.9 all-gather.2
  164.4 54.9 all-reduce.1
where the time goes:
time: 229 us
  waiting for transfers between devices  142 us (62%)
  starting transfers between devices  44 us (19%)
  other arithmetic  18.3 us (8%)
  between operations  14.9 us (7%)
  local copies, waits for them, and re-layouts  9.72 us (4%)
    psum x1, waiting for transfers between devices, on_device(): weighted_new = lax.psum(node_weight * force_new, 'node')  55.1 us
    all_gather x1, waiting for transfers between devices, on_device(): shard_piece = lax.all_gather(force_old[None], 'node', axis=0, tiled=True)  38.3 us
    ppermute x5, starting transfers between devices, padded_2(): lax.ppermute(lax.slice_in_dim(block, 0, width, axis=dim), axis, backward)  27.7 us
    ppermute x5, waiting for transfers between devices, padded_2(): lax.ppermute(lax.slice_in_dim(block, block.shape[dim] - width, None, axis...  26.4 us
    ppermute x1, waiting for transfers between devices, shifted_2(): return lax.ppermute(array, axis, pairs)  20.7 us
    ppermute x5, starting transfers between devices, padded_2(): lax.ppermute(lax.slice_in_dim(block, block.shape[dim] - width, None, axis...  13.9 us
    div x4, other arithmetic, on_device(): iterate = (right_side + implicit * neighbour_sum(widened)) / divisor  6.12 us
    slice x10, local copies, waits for them, and re-layouts, neighbour_sum(): total = total + jnp.roll(inner, -1, 2) + jnp.roll(inner, 1, 2)  5.54 us
  transfers between devices with their start and end apart: 13, of which 11 were waited for; matrix products, arithmetic and copies ran while one was open for 2% of the time, Pallas kernels for 0%

commit v1 on v0

v1 whole, which is shorter than its diff:
```python
import jax
import jax.numpy as jnp
from jax import lax
from jax.experimental import pallas as pl
from jax.experimental.pallas import tpu as pltpu
from jax.sharding import PartitionSpec as P

NODES = 4
time_step = 0.25
diffusion = 4.0
reaction = 1.0
MESH = pl.DeviceIdType.MESH
H = 4
NMSG = 80


def collocation(count):
    points = [-0.8611363115940526, -0.3399810435848563, 0.3399810435848563, 0.8611363115940526]
    raw_weights = [0.3478548451374538, 0.6521451548625461, 0.6521451548625461, 0.3478548451374538]
    node_times = [(point + 1.0) / 2.0 for point in points]
    quadrature = [[0.0 for column in range(count)] for target in range(count)]
    for source in range(count):
        coeffs = [1.0]
        scaling = 1.0
        for other in range(count):
            if other != source:
                other_time = node_times[other]
                shifted = [0.0] + coeffs
                for power in range(len(coeffs)):
                    shifted[power] = shifted[power] - other_time * coeffs[power]
                coeffs = shifted
                scaling = scaling * (node_times[source] - other_time)
        for target in range(count):
            target_time = node_times[target]
            integral = 0.0
            for power in range(len(coeffs)):
                integral = integral + coeffs[power] * target_time ** (power + 1) / (power + 1)
            quadrature[target][source] = integral / scaling
    return (node_times, quadrature, [weight / 2.0 for weight in raw_weights])


TIMES, QUAD, WEIGHTS = collocation(NODES)
IMPLICIT = [time_step * diffusion * t for t in TIMES]
SCALE = [1.0 / (1.0 + 6.0 * a) for a in IMPLICIT]
BETA = [a / (1.0 + 6.0 * a) for a in IMPLICIT]
LINEAR = reaction - 6.0 * diffusion


def pick(table, index):
    value = jnp.float32(table[-1])
    for at in range(len(table) - 2, -1, -1):
        value = jnp.where(index == at, jnp.float32(table[at]), value)
    return value


def flat_ring(x):
    return (pltpu.roll(x, 1, 0) + pltpu.roll(x, x.shape[0] - 1, 0)) + (
        pltpu.roll(x, 1, 1) + pltpu.roll(x, x.shape[1] - 1, 1)
    )


def kernel(spaces, start_ref, x_ref, new_ref, end_ref,
           XB, UB, RB, BG, DA, DB, EO, UX, VB, VR, send, recv, local):
    sp, nd, tm = lax.axis_index("space"), lax.axis_index("node"), lax.axis_index("tm")
    h, c = nd // 2, nd % 2
    zp, zm = (sp + 1) % spaces, (sp + spaces - 1) % spaces
    y = 2 * h + tm

    def at_y(by):
        to = (y + by) % 4
        return (sp, (to // 2) * 2 + c, to % 2)

    SIB = (sp, 2 * h + 1 - c, tm)
    PAR = (sp, 2 * (1 - h) + c, tm)
    ZP, ZM = (zp, nd, tm), (zm, nd, tm)
    YP, YM = at_y(1), at_y(3)

    barrier = pltpu.get_barrier_semaphore()
    for device in (SIB, PAR, ZP, ZM, YP, YM):
        pl.semaphore_signal(barrier, inc=1, device_id=device, device_id_type=MESH)

    own = x_ref.at[0, 0]
    begin_in = start_ref.at[0]
    loads = [pltpu.make_async_copy(own, XB.at[0, pl.ds(H, 8)], local.at[0])]
    loads[0].start()
    begin_load = pltpu.make_async_copy(begin_in, BG.at[pl.ds(3, 8)], local.at[1])

    @pl.when(tm == 0)
    def _():
        begin_load.start()

    pl.semaphore_wait(barrier, 6)

    count = [0]

    def message(src, dst, device):
        at = count[0]
        count[0] += 1
        return pltpu.make_async_remote_copy(
            src_ref=src, dst_ref=dst, send_sem=send.at[at], recv_sem=recv.at[at],
            device_id=device, device_id_type=MESH)

    order = [0, 7, 1, 6, 2, 5, 3, 4]
    f1 = {p: message(own.at[p], XB.at[2, H + p], PAR) for p in order}
    f2 = message(own, XB.at[1, pl.ds(H, 8)], SIB)
    f3 = {p: message(own.at[p], XB.at[0, H + 8 + p if p < 4 else p - 4], ZM if p < 4 else ZP) for p in order}
    for p in order[:2]:
        f1[p].start()
    f2.start()
    for p in order[:2]:
        f3[p].start()
    for p in order[2:]:
        f1[p].start()
        f3[p].start()
    b0 = message(begin_in.at[pl.ds(c * 5, 3)], BG.at[pl.ds((1 - c) * 11, 3)],
                 (jnp.where(c == 0, zm, zp), nd, tm))

    @pl.when(tm == 0)
    def _():
        b0.start()

    across = {p: message(XB.at[2, H + p], XB.at[3, H + p], SIB) for p in order}
    along = {p: message(XB.at[2, H + p], XB.at[2, H + 8 + p if p < 4 else p - 4], ZM if p < 4 else ZP) for p in order}
    rim = lambda p: H + 8 + p if p < 4 else p - 4
    own_rim = {p: message(XB.at[0, rim(p)], XB.at[1, rim(p)], SIB) for p in order}
    far_rim = {p: message(XB.at[2, rim(p)], XB.at[3, rim(p)], SIB) for p in order}
    hs = (1 - c) * 11
    b1 = message(BG.at[pl.ds(hs, 3)], BG.at[pl.ds(hs, 3)], SIB)
    eo, eb = [], []
    for k in range(4):
        p = k + c * (7 - 2 * k)
        rows = pl.ds(h * 64, 64)
        eo.append([message(EO.at[k, rows], BG.at[p + 3, rows], d) for d in (YP, YM)])
        entry = [message(BG.at[p + 3], BG.at[p + 3], SIB)]
        if k < 3:
            entry.append(message(BG.at[p + 3], BG.at[(1 - c) * (11 + k) + c * (2 - k)],
                                 (jnp.where(c == 0, zm, zp), nd, tm)))
        eb.append(entry)

    nodes = [nd, 2 * h + 1 - c, 2 * (1 - h) + c, 2 * (1 - h) + 1 - c]
    targets = [nodes[0], nodes[2]]
    flat = lambda f: [f(m, j) for m in range(NODES) for j in range(NODES)]
    q_u = flat(lambda m, j: time_step * diffusion * SCALE[m] * QUAD[m][j])
    q_r = flat(lambda m, j: time_step * SCALE[m] * QUAD[m][j])
    cu = [[pick(q_u, t * NODES + n) for n in nodes] for t in targets]
    cr = [[pick(q_r, t * NODES + n) for n in nodes] for t in targets]
    cs = [pick(SCALE, t) for t in targets]
    beta = [pick(BETA, t) for t in targets]
    wt = [pick([time_step * w for w in WEIGHTS], n) for n in nodes]
    wx = [wt[0], wt[2]]

    def nonlinear(x):
        return x * (LINEAR - reaction * (x * x))

    def point(i):
        xs = [XB[s, i] for s in range(4)]
        ns = [nonlinear(x) for x in xs]
        for t in range(2):
            UB[t, i] = (cu[t][0] * xs[0] + cu[t][1] * xs[1]) + (cu[t][2] * xs[2] + cu[t][3] * xs[3])
            RB[t, i] = ((cr[t][0] * ns[0] + cr[t][1] * ns[1]) + (cr[t][2] * ns[2] + cr[t][3] * ns[3])) - cs[t] * xs[2 * t]

    def end_old(k):
        p = k + c * (7 - 2 * k)
        i = p + H
        mix = lambda i: (wt[0] * XB[0, i] + wt[1] * XB[1, i]) + (wt[2] * XB[2, i] + wt[3] * XB[3, i])
        u = mix(i)
        total = mix(i - 1) + mix(i + 1) + flat_ring(u)
        rest = BG[p + 3]
        for s in range(4):
            rest = rest + wt[s] * nonlinear(XB[s, i])
        EO[k] = rest + diffusion * total

    loads[0].wait()

    @pl.when(tm == 0)
    def _():
        begin_load.wait()

    f2.wait_recv()
    for k in range(5):
        if k < 4:
            pair = (k, 7 - k)
            for p in pair:
                f1[p].wait_recv()
                across[p].start()
                along[p].start()
            for p in pair:
                f3[p].wait_recv()
                own_rim[p].start()
            for p in pair:
                across[p].wait_recv()
                point(H + p)
        if k > 0:
            pair = (k - 1, 8 - k)
            for p in pair:
                along[p].wait_recv()
                far_rim[p].start()

            if k == 1:
                @pl.when(tm == 0)
                def _():
                    b0.wait_recv()
                    b1.start()
            for p in pair:
                own_rim[p].wait_recv()
                far_rim[p].wait_recv()
                point(rim(p))

            @pl.when(tm == 0)
            def _():
                end_old(k - 1)
                for m in eo[k - 1]:
                    m.start()

    @pl.when(tm == 1)
    def _():
        for k in range(4):
            for m in eo[k]:
                m.wait_recv()
            for m in eb[k]:
                m.start()
        for k in range(3):
            eb[k][1].wait_recv()
        b1.start()
        for k in range(4):
            eb[k][0].wait_recv()

    b1.wait_recv()

    def first(j, carry):
        for t in range(2):
            u = UB[t, j + 1]
            DA[t, j] = (RB[t, j + 1] + cs[t] * BG[j]) + ((UB[t, j] + UB[t, j + 2]) + flat_ring(u))
        return carry

    lax.fori_loop(0, 14, first, 0)

    def stage(src, dst):
        def body(j, carry):
            for t in range(2):
                d = src[t, j]
                dst[t, j] = DA[t, j] + beta[t] * ((src[t, j - 1] + src[t, j + 1]) + flat_ring(d))
            return carry
        return body

    DC = UB
    lax.fori_loop(1, 13, stage(DA, DB), 0)
    lax.fori_loop(2, 12, stage(DB, DC), 0)

    def last(j, carry):
        total = None
        for t in range(2):
            d = DC[t, j]
            x = XB[2 * t, j + 1] + (DA[t, j] + beta[t] * ((DC[t, j - 1] + DC[t, j + 1]) + flat_ring(d)))
            DB[t, j] = x
            total = wx[t] * x if total is None else total + wx[t] * x
        UX[j - 2] = total
        return carry

    edge = [message(UX.at[1], UX.at[9], ZM), message(UX.at[8], UX.at[0], ZP)]
    for j in (3, 10):
        last(j, 0)
    for m in edge:
        m.start()
    lax.fori_loop(4, 10, last, 0)
    out_new = pltpu.make_async_copy(DB.at[0, pl.ds(3, 8)], new_ref.at[0, 0], local.at[2])
    out_new.start()

    def force(p):
        u = UX[p + 1]
        VB[p] = (wx[0] * nonlinear(DB[0, p + 3]) + wx[1] * nonlinear(DB[1, p + 3])) + diffusion * (
            (UX[p] + UX[p + 2]) + flat_ring(u))

    swap = [message(VB.at[pl.ds(1, 6)], VR.at[pl.ds(1, 6)], SIB),
            message(VB.at[0], VR.at[0], SIB), message(VB.at[7], VR.at[7], SIB)]

    def inner(p, carry):
        force(p)
        return carry

    lax.fori_loop(1, 7, inner, 0)
    swap[0].start()
    for m in edge:
        m.wait_recv()
    force(0)
    force(7)
    swap[1].start()
    swap[2].start()

    def finish(p, carry):
        VB[p + 8] = BG[p + 3] + (VB[p] + VR[p])
        return carry

    for m in swap:
        m.wait_recv()
    lax.fori_loop(0, 8, finish, 0)
    out_end = pltpu.make_async_copy(VB.at[pl.ds(8, 8)], end_ref.at[0], local.at[3])
    out_end.start()
    for m in list(f1.values()) + [f2] + list(f3.values()) + list(across.values()) + list(along.values()) \
            + list(own_rim.values()) + list(far_rim.values()) + [b1] + edge + swap:
        m.wait_send()

    @pl.when(tm == 0)
    def _():
        b0.wait_send()
        for k in range(4):
            for m in eo[k]:
                m.wait_send()

    @pl.when(tm == 1)
    def _():
        for k in range(4):
            for m in eb[k]:
                m.wait_send()

    out_new.wait()
    out_end.wait()
    assert count[0] <= NMSG


def on_device(spaces, start_old, nodes_old):
    import functools
    plane = (128, 256)
    V = lambda *lead: pltpu.VMEM(lead + plane, jnp.float32)
    new, end = pl.pallas_call(
        functools.partial(kernel, spaces),
        out_shape=(jax.ShapeDtypeStruct(nodes_old.shape, jnp.float32),
                   jax.ShapeDtypeStruct(start_old.shape, jnp.float32)),
        in_specs=[pl.BlockSpec(memory_space=pl.ANY)] * 2,
        out_specs=(pl.BlockSpec(memory_space=pl.ANY),) * 2,
        scratch_shapes=[V(4, 16), V(2, 16), V(2, 16), V(14), V(2, 14), V(2, 14), V(4), V(10), V(16), V(8),
                        pltpu.SemaphoreType.DMA((NMSG,)), pltpu.SemaphoreType.DMA((NMSG,)),
                        pltpu.SemaphoreType.DMA((4,))],
        compiler_params=pltpu.CompilerParams(collective_id=0, has_side_effects=True),
    )(start_old, nodes_old)
    return new, end


def solution(mesh):
    import functools
    return jax.shard_map(
        functools.partial(on_device, mesh.shape["space"]),
        mesh=mesh,
        in_specs=(P("tm", "space", None, None), P("tm", "node", "space", None, None)),
        out_specs=(P("tm", "node", "space", None, None), P("tm", "space", None, None)),
        check_vma=False,
    )
```

time: 229 us -> 77.4 us (0.34)
  the two profiles are of different devices: /device:TPU:1 before, /device:TPU:9 now
where the time goes in v1:
time: 77.4 us; the launch traced here: 77.1 us
  Pallas kernels  73.1 us (94%)
  local copies, waits for them, and re-layouts  3.33 us (4%)
    pallas_call x1, Pallas kernels, on_device(): pl.pallas_call(functools.partial(kernel, spaces), out_shape=(jax.ShapeDty...  73.1 us
    unnamed x4, local copies, waits for them, and re-layouts  3.33 us

profile of v1, /device:TPU:9, one launch (start us, length us, event | category | flops | bytes accessed | tf_op | source)
XLA Modules:
  0.0 77.1 jit_solution(5323819418632278966)
XLA Ops:
  0.6 73.1 %shard_map.41 = (f32[1,1,8,128,256]{4,3,2,1,0:T(8,128)}, f32[1,8,128,256]{3,2,1,0:T(8,128)}) custom-call(f32[1,8,128,256]{3,2,1,0:T(8,128)} %start_ref.1, f32[1,1,8,128,256]{4,3,2,1,0:T(8,128)} %x_ref.1), custom_call_target="tpu_custom_call" | custom-call | tf_op jit(solution)/shard_map/pallas_call | solution.py:325
  73.7 0.0 copy-start
  73.7 2.4 %copy.6 = f32[1,1,8,128,256]{4,3,2,1,0:T(8,128)} copy(f32[1,1,8,128,256]{4,3,2,1,0:T(8,128)} %get-tuple-element.4) | data formatting | bytes 2097152
  76.1 0.0 copy-done
  76.1 1.0 %copy.7 = f32[1,8,128,256]{3,2,1,0:T(8,128)} copy(f32[1,8,128,256]{3,2,1,0:T(8,128)S(1)} %copy-done) | data formatting | bytes 2097152
Async XLA Ops:
  73.7 2.4 %copy-start = (f32[1,8,128,256]{3,2,1,0:T(8,128)S(1)}, f32[1,8,128,256]{3,2,1,0:T(8,128)}, u32[]{:S(2)}) copy-start(f32[1,8,128,256]{3,2,1,0:T(8,128)} %get-tuple-element.5) | copy-start | bytes 3145732
